TPU v7x, 128 devices: a whole 4x4x4 slice. The times are simulated.
128 devices in a mesh: dp: 64 (over x, z_hi, y, core), tensor: 2 (over z_lo).
Axes of the slice: x: 4, y: 4, z: 4 (z_hi: 2, z_lo: 2; z = z_hi * 2 + z_lo), core: 2. Of those that a mesh axis runs over, the one named last changes fastest.
Arguments:
- inputs: bfloat16 [16384, 1152], P(('dp', 'tensor')), may hold values from -24 to 24
- doc_ids: int32 [64, 256], P('dp'), may hold values from 0 to 3, never falling along the last dimension, each value on 1 to 128 neighbouring positions
- prenorm: bfloat16 [1152], P('dp'), may hold values from 0.099609375 to 1.8984375
- query_proj: bfloat16 [1152, 1024], P('dp', 'tensor'), may hold values from -0.1875 to 0.1875
- key_proj: bfloat16 [1152, 256], P('dp'), may hold values from -0.1875 to 0.1875
- value_proj: bfloat16 [1152, 256], P('dp'), may hold values from -0.1875 to 0.1875
- querynorm: bfloat16 [256], P('dp'), may hold values from 0.5 to 2
- keynorm: bfloat16 [256], P('dp'), may hold values from 0.5 to 2
- output_proj: bfloat16 [1024, 1152], P('tensor', 'dp'), may hold values from -0.1875 to 0.1875
- postnorm: bfloat16 [1152], P('dp'), may hold values from 0.099609375 to 1.8984375
- ffnnorm: bfloat16 [1152], P('dp'), may hold values from 0.099609375 to 1.8984375
- gate_proj: bfloat16 [1152, 6912], P('dp', 'tensor'), may hold values from -0.1875 to 0.1875
- up_proj: bfloat16 [1152, 6912], P('dp', 'tensor'), may hold values from -0.1875 to 0.1875
- down_proj: bfloat16 [6912, 1152], P('tensor', 'dp'), may hold values from -0.078125 to 0.078125
- endnorm: bfloat16 [1152], P('dp'), may hold values from 0.099609375 to 1.8984375
- cotangent: bfloat16 [16384, 1152], P(('dp', 'tensor')), may hold values from -24 to 24
Outputs:
- layer_out: bfloat16 [16384, 1152], P(('dp', 'tensor'))
- inputs_grad: float32 [16384, 1152], P(('dp', 'tensor'))
- prenorm_grad: float32 [1152], P('dp')
- query_grad: float32 [1152, 1024], P('dp', 'tensor')
- key_grad: float32 [1152, 256], P('dp')
- value_grad: float32 [1152, 256], P('dp')
- querynorm_grad: float32 [256], P('dp')
- keynorm_grad: float32 [256], P('dp')
- output_grad: float32 [1024, 1152], P('tensor', 'dp')
- postnorm_grad: float32 [1152], P('dp')
- ffnnorm_grad: float32 [1152], P('dp')
- gate_grad: float32 [1152, 6912], P('dp', 'tensor')
- up_grad: float32 [1152, 6912], P('dp', 'tensor')
- down_grad: float32 [6912, 1152], P('tensor', 'dp')
- endnorm_grad: float32 [1152], P('dp')
Inputs may be any that keep to these rules, and one draw needn't show every extreme that they name: `doc_ids`: in each sequence the document numbers never fall; every one of the 4 documents has 1 to half of 256 tokens, and some document has exactly half of 256 tokens.
All inputs are finite; a program needn't handle non-finite values.
Results may differ from a plain program's by a relative error of at most 0.025.
Values may be sent and summed in bfloat16 or wider, within the bound.
No kernel may reach another device: no remote copies, remote signals or barrier semaphores. Data moves between devices by JAX's collectives and lax.ppermute only.
A program may use at most 256 MiB of HBM per device.

v0:
```python
from functools import partial
import math
import jax
import jax.numpy as jnp
from jax import lax
from jax.sharding import PartitionSpec as P

H = 4
HD = 256
epsilon = 1e-06
rope_base = 1000000.0
query_scale = 0.0625


def sent_together(arrays, axis, dim, along):
    both = jnp.concatenate(arrays, axis=along)
    whole, at, gathered = (lax.all_gather(both, axis, axis=dim, tiled=True), 0, [])
    for a in arrays:
        gathered.append(lax.slice_in_dim(whole, at, at + a.shape[along], axis=along))
        at += a.shape[along]
    return tuple(gathered)


def gather_turned(arrays, axis, dims):
    turned = [jnp.moveaxis(a, dim, 0) for a, dim in zip(arrays, dims)]
    widths = [t[0].size for t in turned]
    both = jnp.concatenate([t.reshape(-1, w) for t, w in zip(turned, widths)], axis=1)
    whole = lax.all_gather(both, axis, axis=0, tiled=True)
    tiles = jnp.split(whole, [sum(widths[:k]) for k in range(1, len(widths))], axis=1)
    return tuple(
        (
            jnp.moveaxis(b.reshape(-1, *t.shape[1:]), 0, dim)
            for b, t, dim in zip(tiles, turned, dims)
        )
    )


def rms_scale(values, scales):
    mean_sq = jnp.mean(values * values, axis=-1, keepdims=True)
    return values * lax.rsqrt(mean_sq + epsilon) * scales


def head_piece(cos_tab, sin_tab, factor, raw_heads, scales):
    normed = rms_scale(raw_heads, scales)
    half_width = normed.shape[-1] // 2
    first_half = normed[..., :half_width]
    second = normed[..., half_width:]
    cos_rows = cos_tab[:, None, :]
    sin_rows = sin_tab[:, None, :]
    turned = jnp.concatenate(
        [first_half * cos_rows - second * sin_rows, second * cos_rows + first_half * sin_rows],
        axis=-1,
    )
    return turned * factor


def gelu_mix(gate_in, up_in):
    return jax.nn.gelu(gate_in, approximate=True) * up_in


def matmul(left_op, right_op):
    return jnp.dot(left_op, right_op, preferred_element_type=jnp.float32)


def matmul_nt(left_op, right_op):
    return lax.dot_general(
        left_op, right_op, (((1,), (1,)), ((), ())), preferred_element_type=jnp.float32
    )


def matmul_tn(left_op, right_op):
    return lax.dot_general(
        left_op, right_op, (((0,), (0,)), ((), ())), preferred_element_type=jnp.float32
    )


def rope_tables(segment):
    seq_length = segment.shape[0]
    token_index = jnp.arange(seq_length, dtype=jnp.int32)
    same_doc = segment[:, None] == segment[None, :]
    earlier = token_index[None, :] < token_index[:, None]
    position = jnp.sum(jnp.where(same_doc & earlier, 1, 0).astype(jnp.int32), axis=1).astype(
        jnp.float32
    )
    freq_rates = jnp.exp(jnp.arange(HD // 2, dtype=jnp.float32) * (-2.0 * math.log(rope_base) / HD))
    angles = position[:, None] * freq_rates[None, :]
    allowed = same_doc & (token_index[None, :] <= token_index[:, None])
    return (jnp.cos(angles), jnp.sin(angles), allowed)


def widen_rows(local_rows):
    return lax.all_gather(local_rows, "tensor", axis=0, tiled=True)


def narrow_rows(partial_rows):
    return lax.psum_scatter(partial_rows, "tensor", scatter_dimension=0, tiled=True)


def on_device(
    inputs,
    doc_ids,
    prenorm,
    query_proj,
    key_proj,
    value_proj,
    querynorm,
    keynorm,
    output_proj,
    postnorm,
    ffnnorm,
    gate_proj,
    up_proj,
    down_proj,
    endnorm,
    cotangent,
):
    tensor_size = lax.axis_size("tensor")
    local_heads = H // tensor_size
    seq_length = doc_ids.shape[1]
    kv_share = 1.0 / tensor_size
    width_rows = prenorm.shape[0]
    head_rows = querynorm.shape[0]
    attn_set = (
        *sent_together((query_proj, key_proj, value_proj), "dp", 0, 1),
        lax.all_gather(output_proj, "dp", axis=1, tiled=True),
        lax.all_gather(prenorm, "dp", axis=0, tiled=True),
        lax.all_gather(querynorm, "dp", axis=0, tiled=True),
        lax.all_gather(keynorm, "dp", axis=0, tiled=True),
        lax.all_gather(postnorm, "dp", axis=0, tiled=True),
    )
    ffn_set = ()
    query_all, key_all, value_all, out_all = (attn_set[0], attn_set[1], attn_set[2], attn_set[3])
    pre_gain = attn_set[4].astype(jnp.float32)
    qgain = attn_set[5].astype(jnp.float32)
    kgain = attn_set[6].astype(jnp.float32)
    post_gain = attn_set[7].astype(jnp.float32)
    cos_tab, sin_tab, allowed = rope_tables(doc_ids[0])
    mask_rows = jnp.repeat(allowed, local_heads, axis=0)
    resid = inputs.astype(jnp.float32)
    normed_f, in_back = jax.vjp(rms_scale, resid, pre_gain)
    normed_in = widen_rows(normed_f.astype(jnp.bfloat16))
    q_raw = matmul(normed_in, query_all).reshape(seq_length, local_heads, HD)
    k_raw = matmul(normed_in, key_all).reshape(seq_length, 1, HD)
    values_b = matmul(normed_in, value_all).astype(jnp.bfloat16)
    q_full, q_back = jax.vjp(partial(head_piece, cos_tab, sin_tab, query_scale), q_raw, qgain)
    k_full, k_back = jax.vjp(partial(head_piece, cos_tab, sin_tab, 1.0), k_raw, kgain)
    query_rows = q_full.astype(jnp.bfloat16).reshape(seq_length * local_heads, HD)
    keys_b = k_full[:, 0, :].astype(jnp.bfloat16)
    scores = matmul_nt(query_rows, keys_b)
    exp_scores = jnp.where(mask_rows, jnp.exp(scores), 0.0)
    log_total = jnp.log(jnp.sum(exp_scores, axis=1, keepdims=True))
    probs_b = jnp.where(mask_rows, jnp.exp(scores - log_total), 0.0).astype(jnp.bfloat16)
    mixed_rows = matmul(probs_b, values_b).astype(jnp.bfloat16)
    mixed = mixed_rows.reshape(seq_length, local_heads * HD)
    branch = narrow_rows(matmul(mixed, out_all))
    attn_norm, attn_back = jax.vjp(rms_scale, branch, post_gain)
    hidden = resid + attn_norm
    ffn_set = gather_turned(
        (gate_proj, up_proj, down_proj, ffnnorm, endnorm), "dp", (0, 0, 1, 0, 0)
    )
    gate_all, up_all, down_all = (ffn_set[0], ffn_set[1], ffn_set[2])
    ffn_gain = ffn_set[3].astype(jnp.float32)
    end_gain = ffn_set[4].astype(jnp.float32)
    ff_norm, ff_in_back = jax.vjp(rms_scale, hidden, ffn_gain)
    ff_input = widen_rows(ff_norm.astype(jnp.bfloat16))
    gate_f = matmul(ff_input, gate_all)
    up_f = matmul(ff_input, up_all)
    product, mix_back = jax.vjp(gelu_mix, gate_f, up_f)
    act = product.astype(jnp.bfloat16)
    ff_branch = narrow_rows(matmul(act, down_all))
    end_norm, end_back = jax.vjp(rms_scale, ff_branch, end_gain)
    layer_out = (hidden + end_norm).astype(jnp.bfloat16)
    grad_out = cotangent.astype(jnp.float32)
    d_ff, grad_end = end_back(grad_out)
    d_ff_rows = widen_rows(d_ff.astype(jnp.bfloat16))
    d_act = matmul_nt(d_ff_rows, down_all)
    d_gate, d_up = mix_back(d_act)
    d_gate_b = d_gate.astype(jnp.bfloat16)
    d_up_b = d_up.astype(jnp.bfloat16)
    hidden_cols = d_gate_b.shape[1]
    ff_sums = lax.psum_scatter(
        jnp.concatenate(
            [matmul_tn(ff_input, d_gate_b), matmul_tn(ff_input, d_up_b), matmul_tn(d_ff_rows, act)],
            axis=1,
        ),
        "dp",
        scatter_dimension=0,
        tiled=True,
    )
    sent_gate = ff_sums[:, :hidden_cols]
    sent_up = ff_sums[:, hidden_cols : 2 * hidden_cols]
    sent_down = ff_sums[:, 2 * hidden_cols :].T
    d_ff_input = narrow_rows(matmul_nt(d_gate_b, gate_all) + matmul_nt(d_up_b, up_all))
    d_h_part, grad_ffn = ff_in_back(d_ff_input)
    d_hidden = grad_out + d_h_part
    d_branch, grad_post = attn_back(d_hidden)
    d_branch_rows = widen_rows(d_branch.astype(jnp.bfloat16))
    outw_t = matmul_tn(d_branch_rows, mixed)
    d_mixed = matmul_nt(d_branch_rows, out_all).astype(jnp.bfloat16)
    d_mixed_rows = d_mixed.reshape(seq_length * local_heads, HD)
    delta = jnp.sum(
        d_mixed_rows.astype(jnp.float32) * mixed_rows.astype(jnp.float32), axis=1, keepdims=True
    )
    again = matmul_nt(query_rows, keys_b)
    probs_f = jnp.where(mask_rows, jnp.exp(again - log_total), 0.0)
    d_probs = matmul_nt(d_mixed_rows, values_b)
    d_scores = (probs_f * (d_probs - delta)).astype(jnp.bfloat16)
    d_queries = matmul(d_scores, keys_b).reshape(seq_length, local_heads, HD)
    keys_part = matmul_tn(d_scores, query_rows)
    values_part = matmul_tn(probs_f.astype(jnp.bfloat16), d_mixed_rows)
    d_keys, d_values = (
        lax.psum(keys_part.astype(jnp.bfloat16), "tensor").astype(jnp.float32),
        lax.psum(values_part.astype(jnp.bfloat16), "tensor").astype(jnp.float32),
    )
    d_q_raw, grad_qgain = q_back(d_queries)
    d_k_raw, grad_kgain = k_back(d_keys[:, None, :])
    d_q_b = d_q_raw.reshape(seq_length, local_heads * HD).astype(jnp.bfloat16)
    d_k_b = d_k_raw.reshape(seq_length, HD).astype(jnp.bfloat16)
    d_v_b = d_values.astype(jnp.bfloat16)
    grad_query = matmul_tn(normed_in, d_q_b)
    grad_key = matmul_tn(normed_in, d_k_b)
    grad_value = matmul_tn(normed_in, d_v_b)
    d_normed = matmul_nt(d_q_b, query_all) + kv_share * (
        matmul_nt(d_k_b, key_all) + matmul_nt(d_v_b, value_all)
    )
    d_in_part, grad_pre = in_back(narrow_rows(d_normed))
    inputs_grad = d_hidden + d_in_part
    gain_pre, gain_post, gain_ffn, gain_end, gain_q, gain_k = lax.psum(
        (grad_pre, grad_post, grad_ffn, grad_end, grad_qgain, kv_share * grad_kgain),
        ("dp", "tensor"),
    )
    dp_index = lax.axis_index("dp")
    sent_pre = lax.dynamic_slice_in_dim(gain_pre, dp_index * width_rows, width_rows)
    sent_post = lax.dynamic_slice_in_dim(gain_post, dp_index * width_rows, width_rows)
    sent_ffn = lax.dynamic_slice_in_dim(gain_ffn, dp_index * width_rows, width_rows)
    sent_end = lax.dynamic_slice_in_dim(gain_end, dp_index * width_rows, width_rows)
    sent_qgain = lax.dynamic_slice_in_dim(gain_q, dp_index * head_rows, head_rows)
    sent_kgain = lax.dynamic_slice_in_dim(gain_k, dp_index * head_rows, head_rows)
    query_cols = grad_query.shape[1]
    out_cols = outw_t.shape[1]
    flat_query, flat_key, flat_value, flat_outw = (
        lax.psum_scatter(grad_query.reshape(-1), "dp", scatter_dimension=0, tiled=True),
        lax.psum_scatter(grad_key.reshape(-1), "dp", scatter_dimension=0, tiled=True),
        lax.psum_scatter(grad_value.reshape(-1), "dp", scatter_dimension=0, tiled=True),
        lax.psum_scatter(outw_t.reshape(-1), "dp", scatter_dimension=0, tiled=True),
    )
    sent_query = flat_query.reshape(width_rows, query_cols)
    sent_key = flat_key.reshape(width_rows, HD)
    sent_value = flat_value.reshape(width_rows, HD)
    sent_outw = flat_outw.reshape(width_rows, out_cols).T
    return (
        layer_out,
        inputs_grad,
        sent_pre,
        sent_query,
        sent_key,
        sent_value,
        sent_qgain,
        sent_kgain,
        sent_outw,
        sent_post,
        sent_ffn,
        sent_gate,
        sent_up,
        sent_down,
        sent_end,
    )


def solution(mesh):
    return jax.shard_map(
        on_device,
        mesh=mesh,
        in_specs=(
            P(("dp", "tensor"), None),
            P("dp", None),
            P("dp"),
            P("dp", "tensor"),
            P("dp", None),
            P("dp", None),
            P("dp"),
            P("dp"),
            P("tensor", "dp"),
            P("dp"),
            P("dp"),
            P("dp", "tensor"),
            P("dp", "tensor"),
            P("tensor", "dp"),
            P("dp"),
            P(("dp", "tensor"), None),
        ),
        out_specs=(
            P(("dp", "tensor"), None),
            P(("dp", "tensor"), None),
            P("dp"),
            P("dp", "tensor"),
            P("dp", None),
            P("dp", None),
            P("dp"),
            P("dp"),
            P("tensor", "dp"),
            P("dp"),
            P("dp"),
            P("dp", "tensor"),
            P("dp", "tensor"),
            P("tensor", "dp"),
            P("dp"),
        ),
        check_vma=False,
    )
```

profile of v0, /device:TPU:0, one launch (start us, length us, event | category | flops | bytes accessed | tf_op | source)
XLA Modules:
  0.0 1494.3 jit_solution(17384775213538259779)
XLA Ops:
  8.0 1.4 maximum_bitcast_fusion.4
  9.4 1.3 fusion.93
  16.4 175.6 %all-reduce.15 = (bf16[1152]{0:T(1024)(128)(2,1)S(1)}, bf16[256]{0:T(256)(128)(2,1)S(1)}, bf16[256]{0:T(256)(128)(2,1)S(1)}, bf16[1152]{0:T(1024)(128)(2,1)}) all-reduce(bf16[1152]{0:T(1024)(128)(2,1)S(1)} %dynamic-update-slice, bf16[256]{0:T(256)(128)(2,1)S(1)} %dynamic-update-slice.2, ...), channel_id=1, replica_groups=mesh['dp'=64,'tensor'=2] {'dp'}, use_global_device_ids=true, to_apply=%add.4 | all-reduce | flops 2816 | bytes 11264
  196.8 7.4 all_gather.34
  204.2 1.2 multiply_cosine_fusion.1
  205.5 3.1 reshape.393
  208.5 2.9 reshape.391
  212.5 1.6 multiply_reduce_fusion.11
  214.1 1.3 fusion.29
  215.4 1.4 reshape.362
  219.8 1.9 fusion.66
  223.4 1.8 multiply_subtract_fusion
  225.2 1.8 copy.79
  227.0 1.8 copy.80
  228.7 1.4 select_reduce_fusion
  230.9 2.0 convolution_convert_fusion.1
  232.9 1.8 copy.81
  235.9 3.0 fusion.94
  241.4 16.2 %reduce-scatter.5.cloned.1.call-done = f32[128,1152]{1,0:T(8,128)} async-done(((f32[256,1152]{1,0:T(8,128)}), f32[128,1152]{1,0:T(8,128)}) %reduce-scatter.5.cloned.1.call-update) | async-done | bytes 589840 | tf_op jit(solution)/shard_map/reduce_scatter | solution.py:96
  257.6 1.2 multiply_reduce_fusion.6
  258.8 1.3 multiply_reduce_fusion.5
  260.2 156.6 %all-gather.11.cloned.1.call-done = bf16[64,18,10370]{2,1,0:T(8,128)(2,1)} async-done(((bf16[1,18,10370]{2,1,0:T(8,128)(2,1)}), bf16[64,18,10370]{2,1,0:T(8,128)(2,1)}) %all-gather.11.cloned.1.call-update) | async-done | bytes 23892496 | tf_op jit(solution)/shard_map/all_gather | solution.py:28
  416.8 28.7 %reshape.395 = bf16[1152,10370]{1,0:T(8,128)(2,1)} reshape(bf16[64,18,10370]{2,1,0:T(8,128)(2,1)} %all-gather.11.cloned.1.call-done) | data formatting | bytes 47784960
  445.5 2.0 convert_reduce_fusion
  447.7 10.3 all_gather.41
  458.0 7.9 fusion.10
  465.8 3.8 copy-done
  469.6 6.1 multiply_convert_fusion.1
  475.7 5.1 fusion.2
  480.8 22.0 %reduce-scatter.7.cloned.1.call-done = f32[128,1152]{1,0:T(8,128)} async-done(((f32[256,1152]{1,0:T(8,128)}), f32[128,1152]{1,0:T(8,128)}) %reduce-scatter.7.cloned.1.call-update) | async-done | bytes 589840 | tf_op jit(solution)/shard_map/reduce_scatter | solution.py:96
  502.8 1.2 multiply_reduce_fusion.4
  504.0 1.9 fusion.38
  505.9 2.3 fusion.39
  508.2 9.4 all_gather.42
  517.7 10.4 fusion.18
  528.1 1.2 slice-done.4
  530.2 4.1 fusion.4
  534.3 5.1 fusion.21
  539.6 9.8 fusion.97
  549.4 7.8 fusion.95
  557.3 9.0 fusion.96
  566.3 1.9 multiply_reduce_fusion
  568.9 2.2 multiply_reduce_fusion.1
  571.9 8.5 all_gather.43
  581.8 2.2 convolution_convert_fusion.2
  585.2 1.5 fusion.25
  586.7 2.0 fusion.26
  590.9 1.3 multiply_reduce_fusion.7
  593.0 1.5 fusion.44
  594.5 1.5 fusion.27
  596.0 29.6 %all-reduce.22.cloned.1.call-done = (bf16[256,1,256]{0,2,1:T(8,128)(2,1)}, bf16[256,256]{1,0:T(8,128)(2,1)}) async-done(((bf16[256,1,256]{0,2,1:T(8,128)(2,1)}, bf16[256,256]{1,0:T(8,128)(2,1)}), (bf16[256,1,256]{0,2,1:T(8,128)(2,1)}, bf16[256,256]{1,0:T(8,128)(2,1)})) %all-reduce.22.cloned.1.call-update) | async-done | bytes 262160 | tf_op jit(solution)/shard_map/psum | solution.py:212
  626.6 1.2 fusion.69
  627.8 1.7 fusion.54
  632.3 1.4 fusion.20
  634.0 32.7 %pad_maximum_fusion = f32[1152,10368]{1,0:T(8,128)} fusion(f32[1152,3456]{1,0:T(8,128)} %fusion.97, f32[1152,3456]{1,0:T(8,128)} %fusion.96, f32[1152,3456]{1,0:T(8,128)} %fusion.95), kind=kLoop, calls=%fused_computation | loop fusion | flops 23887872 | bytes 95551488 | tf_op jit(solution)/shard_map/concatenate | solution.py:182
  667.2 2.1 copy.90
  669.9 2.0 copy.93
  672.2 1.6 copy.91
  674.2 1.7 copy.92
  678.1 1.3 fusion.36
  679.4 74.5 %all-reduce.13 = (f32[1152]{0:T(1024)S(1)}, f32[256]{0:T(256)S(1)}, f32[256]{0:T(256)S(1)}, f32[1152]{0:T(1024)S(1)}, f32[1152]{0:T(1024)S(1)}, /*index=5*/f32[1152]{0:T(1024)S(1)}) all-reduce(f32[1152]{0:T(1024)S(1)} %get-tuple-element.25, f32[256]{0:T(256)S(1)} %copy-done.51, ...), channel_id=1, replica_groups=mesh['dp'=64,'tensor'=2] {'dp','tensor'}, use_global_device_ids=true, to_apply=%region_22.23 | all-reduce | flops 5120 | bytes 40960 | tf_op jit(solution)/shard_map/psum | solution.py:228
  757.4 2.1 fusion.41
  759.5 720.0 %all-reduce.20.cloned.1.call-done = (f32[589824]{0:T(1024)}, f32[294912]{0:T(1024)}, f32[294912]{0:T(1024)}, f32[589824]{0:T(1024)}, f32[1152,10368]{1,0:T(8,128)}) async-done(((f32[589824]{0:T(1024)}, f32[294912]{0:T(1024)}, f32[294912]{0:T(1024)}, f32[589824]{0:T(1024)}, f32[1152,10368]{1,0:T(8,128)}), (f32[589824]{0:T(1024)}, f32[294912]{0:T(1024)}, f32[294912]{0:T(1024)}, f32[589824]{0:T(1024)}, ...) | async-done | bytes 54853648
  1485.1 2.5 dynamic-slice_bitcast_fusion
  (221 shorter events, 43.3 us)
Async XLA Ops:
  7.2 198.3 %all-gather.9.cloned.1.call-start = ((), (), s32[]{:S(2)}) async-start(), calls=%async_computation.9 | async-start | bytes 1597440 | tf_op jit(solution)/shard_map/all_gather | solution.py:125
  7.9 200.6 %all-gather.7.cloned.1.call-start = ((), (), s32[]{:S(2)}) async-start(), calls=%async_computation.8 | async-start | bytes 3194880 | tf_op jit(solution)/shard_map/all_gather | solution.py:17
  9.4 248.2 %reduce-scatter.5.cloned.1.call-start = ((), (), s32[]{:S(2)}) async-start(), calls=%async_computation.4 | async-start | bytes 1769472 | tf_op jit(solution)/shard_map/reduce_scatter | solution.py:96
  13.0 206.7 %copy-start.40 = (f32[256]{0:T(256)}, f32[256]{0:T(256)S(1)}, u32[]{:S(2)}) copy-start(f32[256]{0:T(256)S(1)} %convert_element_type.128) | copy-start | bytes 3076
  194.5 35.6 %copy-start.19 = (pred[512,256]{1,0:T(32,128)(4,1)}, pred[512,256]{1,0:T(32,128)(4,1)S(1)}, u32[]{:S(2)}) copy-start(pred[512,256]{1,0:T(32,128)(4,1)S(1)} %reshape.361) | copy-start | bytes 393220
  194.6 16.9 %copy-start.45 = (f32[128]{0:T(128)}, f32[128]{0:T(128)S(1)}, u32[]{:S(2)}) copy-start(f32[128]{0:T(128)S(1)} %multiply_exponential_fusion) | copy-start | bytes 1540
  195.7 15.8 %copy-start.53 = (f32[128]{0:T(128)}, f32[128]{0:T(128)S(1)}, u32[]{:S(2)}) copy-start(f32[128]{0:T(128)S(1)} %fusion.42) | copy-start | bytes 1540
  195.7 15.8 %copy-start.47 = (f32[128]{0:T(128)}, f32[128]{0:T(128)S(1)}, u32[]{:S(2)}) copy-start(f32[128]{0:T(128)S(1)} %fusion.81) | copy-start | bytes 1540
  204.2 9.9 copy-start.2
  218.0 16.7 %copy-start.4 = (f32[256,2,256]{0,2,1:T(8,128)}, f32[256,2,256]{0,2,1:T(8,128)S(1)}, u32[]{:S(2)}) copy-start(f32[256,2,256]{0,2,1:T(8,128)S(1)} %copy.78) | copy-start | bytes 1572868
  222.6 7.5 copy-start.39
  222.6 16.2 %copy-start.32 = (f32[256,2]{0,1:T(2,128)}, f32[256,2]{0,1:T(2,128)S(1)}, u32[]{:S(2)}) copy-start(f32[256,2]{0,1:T(2,128)S(1)} %fusion.79) | copy-start | bytes 6148
  230.2 11.2 copy-start.34
  232.9 8.5 copy-start.50
  232.9 25.9 %copy-start.6 = (bf16[128,1152]{1,0:T(8,128)(2,1)S(1)}, bf16[128,1152]{1,0:T(8,128)(2,1)}, u32[]{:S(2)}) copy-start(bf16[128,1152]{1,0:T(8,128)(2,1)} %param.16) | copy-start | bytes 884740
  235.8 24.4 %copy-start.14 = (bf16[256,512]{1,0:T(8,128)(2,1)}, bf16[256,512]{1,0:T(8,128)(2,1)S(1)}, u32[]{:S(2)}) copy-start(bf16[256,512]{1,0:T(8,128)(2,1)S(1)} %reshape.363) | copy-start | bytes 786436
  235.8 4.6 copy-start.27
  235.8 4.6 copy-start.28
  235.8 4.6 copy-start.29
  238.9 177.9 %all-gather.11.cloned.1.call-start = ((), (), s32[]{:S(2)}) async-start(), calls=%async_computation.10 | async-start | bytes 32747520 | tf_op jit(solution)/shard_map/all_gather | solution.py:28
  241.4 261.4 %reduce-scatter.7.cloned.1.call-start = ((), (), s32[]{:S(2)}) async-start(), calls=%async_computation.5 | async-start | bytes 1769472 | tf_op jit(solution)/shard_map/reduce_scatter | solution.py:96
  241.4 175.4 %copy-start.30 = (f32[1152]{0:T(1024)}, f32[1152]{0:T(1024)S(1)}, u32[]{:S(2)}) copy-start(f32[1152]{0:T(1024)S(1)} %convert_element_type.135) | copy-start | bytes 13828
  258.8 186.7 %copy-start.43 = (f32[128]{0:T(128)}, f32[128]{0:T(128)S(1)}, u32[]{:S(2)}) copy-start(f32[128]{0:T(128)S(1)} %fusion.82) | copy-start | bytes 1540
  260.2 185.3 %copy-start.52 = (f32[128]{0:T(128)}, f32[128]{0:T(128)S(1)}, u32[]{:S(2)}) copy-start(f32[128]{0:T(128)S(1)} %get-tuple-element.47) | copy-start | bytes 1540
  260.2 187.3 %copy-start.46 = (f32[128]{0:T(128)}, f32[128]{0:T(128)S(1)}, u32[]{:S(2)}) copy-start(f32[128]{0:T(128)S(1)} %fusion.83) | copy-start | bytes 1540
  458.0 91.5 %copy-start.8 = (bf16[256,1152]{1,0:T(8,128)(2,1)}, bf16[256,1152]{1,0:T(8,128)(2,1)S(1)}, u32[]{:S(2)}) copy-start(bf16[256,1152]{1,0:T(8,128)(2,1)S(1)} %all_gather.41) | copy-start | bytes 1769476
  458.0 11.6 copy-start
  480.8 85.5 %reduce-scatter.9.cloned.1.call-start = ((), (), s32[]{:S(2)}) async-start(), calls=%async_computation.6 | async-start | bytes 1769472 | tf_op jit(solution)/shard_map/reduce_scatter | solution.py:96
  505.9 22.1 %slice-start = ((s8[24182784]{0:T(1024)(128)(4,1)}), s8[4194304]{0:T(1024)(128)(4,1)S(1)}, s32[]{:S(2)}) async-start(s8[24182784]{0:T(1024)(128)(4,1)} %bitcast.94), calls=%async_computation.13 | async-start | bytes 8388608
  517.6 10.4 copy-start.13
  517.6 10.4 slice-start.1
  517.6 10.4 slice-start.2
  517.6 10.5 slice-start.3
  517.6 11.7 slice-start.4
  517.6 12.6 slice-start.5
  539.4 86.3 %all-reduce.22.cloned.1.call-start = ((), (), s32[]{:S(2)}) async-start(), calls=%async_computation.12 | async-start | bytes 524288 | tf_op jit(solution)/shard_map/psum | solution.py:212
  539.6 9.8 copy-start.21
  549.4 7.8 copy-start.20
  557.3 11.6 copy-start.1
  566.3 4.8 copy-start.56
  566.3 4.8 copy-start.31
  566.3 4.8 copy-start.44
  566.3 14.9 copy-start.12
  571.0 10.7 copy-start.35
  581.7 8.3 copy-start.22
  581.8 9.1 copy-start.5
  581.8 9.1 copy-start.33
  589.9 36.7 %copy-start.41 = (f32[256]{0:T(256)S(1)}, f32[256]{0:T(256)}, u32[]{:S(2)}) copy-start(f32[256]{0:T(256)} %copy-done.40) | copy-start | bytes 3076
  594.5 83.6 %reduce-scatter.11.cloned.1.call-start = ((), (), s32[]{:S(2)}) async-start(), calls=%async_computation.7 | async-start | bytes 1769472 | tf_op jit(solution)/shard_map/reduce_scatter | solution.py:96
  625.6 6.6 copy-start.25
  633.7 33.0 %copy-start.3 = (bf16[256,1152]{1,0:T(8,128)(2,1)S(1)}, bf16[256,1152]{1,0:T(8,128)(2,1)}, u32[]{:S(2)}) copy-start(bf16[256,1152]{1,0:T(8,128)(2,1)} %copy-done.2) | copy-start | bytes 1769476
  633.7 33.0 %copy-start.16 = (bf16[256,2,256]{0,2,1:T(8,128)(2,1)S(1)}, bf16[256,2,256]{0,2,1:T(8,128)(2,1)}, u32[]{:S(2)}) copy-start(bf16[256,2,256]{0,2,1:T(8,128)(2,1)} %fusion.44) | copy-start | bytes 786436
  633.7 845.7 %all-reduce.20.cloned.1.call-start = ((), (), s32[]{:S(2)}) async-start(), calls=%async_computation.11 | async-start | bytes 109707264
  666.7 2.7 copy-start.15
  666.7 2.7 copy-start.18
  669.4 2.5 copy-start.24
  669.9 4.0 copy-start.26
  675.9 2.2 copy-start.48
  675.9 3.5 copy-start.36
  675.9 3.5 copy-start.37
  675.9 3.5 copy-start.38
  675.9 3.5 copy-start.51
  676.0 81.5 %copy-start.54 = (f32[128]{0:T(128)S(1)}, f32[128]{0:T(128)}, u32[]{:S(2)}) copy-start(f32[128]{0:T(128)} %copy-done.53) | copy-start | bytes 1540
  676.0 81.5 %copy-start.10 = (f32[128,1152]{1,0:T(8,128)S(1)}, f32[128,1152]{1,0:T(8,128)}, u32[]{:S(2)}) copy-start(f32[128,1152]{1,0:T(8,128)} %copy-done.9) | copy-start | bytes 1769476
  (8 other events, 9.9 us)
Sparse Core Ops, SparseCore 0:
  11.2 69.4 all-gather.8
  84.5 67.4 all-gather.6
  239.0 18.5 reduce-scatter.4
  261.6 155.1 all-gather.10
  480.9 21.8 reduce-scatter.6
  539.5 25.2 reduce-scatter.8
  594.6 31.0 all-reduce.21
  633.8 25.3 reduce-scatter.10
  676.1 803.3 all-reduce.19
where the time goes:
time: 1500 us; the launch traced here: 1490 us
  waiting for transfers between devices  945 us (63%)
  blocking collectives  286 us (19%)
  matrix products  87.8 us (6%)
  local copies, waits for them, and re-layouts  79.7 us (5%)
  other arithmetic  77 us (5%)
  between operations  18.3 us (1%)
    unnamed x10, waiting for transfers between devices  721 us
    unnamed x1, blocking collectives  176 us
    all_gather x1, waiting for transfers between devices, gather_turned(): whole = lax.all_gather(both, axis, axis=0, tiled=True)  157 us
    psum x1, blocking collectives, on_device(): lax.psum((grad_pre, grad_post, grad_ffn, grad_end, grad_qgain, kv_share *...  74.5 us
    unnamed x146, local copies, waits for them, and re-layouts  59 us
    reduce_scatter x4, waiting for transfers between devices, narrow_rows(): lax.psum_scatter(partial_rows, 'tensor', scatter_dimension=0, tiled=True)  38.2 us
    all_gather x4, blocking collectives, widen_rows(): return lax.all_gather(local_rows, 'tensor', axis=0, tiled=True)  35.6 us
    concatenate x1, other arithmetic, on_device(): jnp.concatenate([matmul_tn(ff_input, d_gate_b), matmul_tn(ff_input, d_up_...  32.7 us
  transfers between devices with their start and end apart: 9, of which 5 were waited for; matrix products, arithmetic and copies ran while one was open for 7% of the time, Pallas kernels for 0%

commit v1 on v0

--- a/solution.py
+++ b/solution.py
@@ -25,7 +25,9 @@
     turned = [jnp.moveaxis(a, dim, 0) for a, dim in zip(arrays, dims)]
     widths = [t[0].size for t in turned]
     both = jnp.concatenate([t.reshape(-1, w) for t, w in zip(turned, widths)], axis=1)
-    whole = lax.all_gather(both, axis, axis=0, tiled=True)
+    whole = jnp.concatenate(
+        lax.all_to_all(jnp.stack([both] * lax.axis_size(axis)), axis, 0, 0), axis=0
+    )
     tiles = jnp.split(whole, [sum(widths[:k]) for k in range(1, len(widths))], axis=1)
     return tuple(
         (

time: 1500 us -> 1790 us (1.19)
  blocking collectives: 286 us -> 678 us
  waiting for transfers between devices: 945 us -> 830 us
    unnamed x1, blocking collectives: 176 us -> 561 us
    all_gather x1 -> x0, waiting for transfers between devices: 157 us -> none  [gather_turned(): whole = lax.all_gather(both, axis, axis=0, tiled=True)]
    reduce_scatter x4, waiting for transfers between devices: 38.2 us -> 78.6 us  [narrow_rows(): lax.psum_scatter(partial_rows, 'tensor', scatter_dimension=0, tiled=True)]
    unnamed x146 -> x175, local copies, waits for them, and re-layouts: 59 us -> 29.4 us
    reshape x0 -> x1, local copies, waits for them, and re-layouts: none -> 28.7 us  [gather_turned(): jnp.concatenate(lax.all_to_all(jnp.stack([both] * lax.axis_size(axis)), a...]
    unnamed x10 -> x9, waiting for transfers between devices: 721 us -> 722 us
  transfers between devices with their start and end apart: 9 -> 9, of which waited for: 5 -> 4; matrix products, arithmetic and copies ran while one was open for 7% -> 6% of each run, Pallas kernels for 0% -> 0%
where the time goes in v1:
time: 1790 us; the launch traced here: 1780 us
  waiting for transfers between devices  830 us (46%)
  blocking collectives  678 us (38%)
  local copies, waits for them, and re-layouts  88.6 us (5%)
  matrix products  83.5 us (5%)
  other arithmetic  70.3 us (4%)
  between operations  18.8 us (1%)
    unnamed x9, waiting for transfers between devices  722 us
    unnamed x1, blocking collectives  561 us
    reduce_scatter x4, waiting for transfers between devices, narrow_rows(): lax.psum_scatter(partial_rows, 'tensor', scatter_dimension=0, tiled=True)  78.6 us
    psum x1, blocking collectives, on_device(): lax.psum((grad_pre, grad_post, grad_ffn, grad_end, grad_qgain, kv_share *...  73.4 us
    all_gather x4, blocking collectives, widen_rows(): return lax.all_gather(local_rows, 'tensor', axis=0, tiled=True)  43.6 us
  transfers between devices with their start and end apart: 9, of which 4 were waited for; matrix products, arithmetic and copies ran while one was open for 6% of the time, Pallas kernels for 0%

profile of v1, /device:TPU:0, one launch (start us, length us, event | category | flops | bytes accessed | tf_op | source)
XLA Modules:
  0.0 1782.3 jit_solution(766103436915816653)
XLA Ops:
  8.7 1.2 concatenate.36
  9.9 10.7 stack.2
  20.7 11.7 all-to-all-start
  37.1 561.4 %all-reduce.15 = (bf16[1152]{0:T(1024)(128)(2,1)S(1)}, bf16[256]{0:T(256)(128)(2,1)S(1)}, bf16[256]{0:T(256)(128)(2,1)S(1)}, bf16[1152]{0:T(1024)(128)(2,1)}) all-reduce(bf16[1152]{0:T(1024)(128)(2,1)S(1)} %dynamic-update-slice, bf16[256]{0:T(256)(128)(2,1)S(1)} %dynamic-update-slice.2, ...), channel_id=1, replica_groups=mesh['dp'=64,'tensor'=2] {'dp'}, use_global_device_ids=true, to_apply=%add.4 | all-reduce | flops 2816 | bytes 11264
  601.2 15.8 all_gather.31
  617.0 1.3 multiply_cosine_fusion.1
  618.2 3.1 reshape.399
  621.3 2.9 reshape.397
  624.8 1.1 reshape.367
  625.9 1.2 copy.78
  627.2 2.2 multiply_reduce_fusion.10
  630.5 1.8 multiply_subtract_fusion
  632.3 1.8 copy.79
  634.1 1.8 copy.80
  637.1 1.3 fusion.66
  638.4 1.5 select_reduce_fusion
  642.3 2.9 fusion.94
  645.3 53.2 %reduce-scatter.5.cloned.1.call-done = f32[128,1152]{1,0:T(8,128)} async-done(((f32[256,1152]{1,0:T(8,128)}), f32[128,1152]{1,0:T(8,128)}) %reduce-scatter.5.cloned.1.call-update) | async-done | bytes 589840 | tf_op jit(solution)/shard_map/reduce_scatter | solution.py:98
  698.5 1.2 multiply_reduce_fusion.6
  699.7 1.3 multiply_reduce_fusion.5
  701.1 28.7 %reshape.371 = bf16[1152,10370]{1,0:T(8,128)(2,1)} reshape(bf16[64,18,10370]{2,1,0:T(8,128)(2,1)} %all-to-all-done) | data formatting | bytes 47784960 | tf_op jit(solution)/shard_map/reshape | solution.py:28
  729.8 2.0 convert_reduce_fusion
  732.0 9.9 all_gather.37
  741.9 7.9 fusion.10
  749.7 3.8 copy-done
  753.5 6.0 multiply_convert_fusion.1
  759.6 5.1 fusion.2
  764.7 25.4 %reduce-scatter.7.cloned.1.call-done = f32[128,1152]{1,0:T(8,128)} async-done(((f32[256,1152]{1,0:T(8,128)}), f32[128,1152]{1,0:T(8,128)}) %reduce-scatter.7.cloned.1.call-update) | async-done | bytes 589840 | tf_op jit(solution)/shard_map/reduce_scatter | solution.py:98
  790.1 1.2 multiply_reduce_fusion.4
  791.3 1.9 fusion.38
  793.2 2.3 fusion.39
  795.5 9.4 all_gather.38
  804.9 10.4 fusion.18
  815.4 1.2 slice-done.4
  817.5 4.0 fusion.4
  821.5 5.1 fusion.21
  826.9 9.8 fusion.97
  836.7 7.9 fusion.95
  844.6 9.0 fusion.96
  853.6 1.9 multiply_reduce_fusion
  856.1 2.2 multiply_reduce_fusion.1
  859.2 8.5 all_gather.39
  869.1 2.2 convolution_convert_fusion.2
  872.5 1.5 fusion.25
  874.0 2.0 fusion.26
  876.1 1.1 convolution_multiply_fusion
  878.3 1.4 multiply_reduce_fusion.7
  880.4 1.5 fusion.44
  881.9 1.5 fusion.27
  883.5 29.6 %all-reduce.22.cloned.1.call-done = (bf16[256,1,256]{0,2,1:T(8,128)(2,1)}, bf16[256,256]{1,0:T(8,128)(2,1)}) async-done(((bf16[256,1,256]{0,2,1:T(8,128)(2,1)}, bf16[256,256]{1,0:T(8,128)(2,1)}), (bf16[256,1,256]{0,2,1:T(8,128)(2,1)}, bf16[256,256]{1,0:T(8,128)(2,1)})) %all-reduce.22.cloned.1.call-update) | async-done | bytes 262160 | tf_op jit(solution)/shard_map/psum | solution.py:214
  914.1 1.2 fusion.69
  915.3 1.7 fusion.54
  917.6 1.1 fusion.71
  919.8 1.4 fusion.20
  921.5 32.7 %pad_maximum_fusion = f32[1152,10368]{1,0:T(8,128)} fusion(f32[1152,3456]{1,0:T(8,128)} %fusion.97, f32[1152,3456]{1,0:T(8,128)} %fusion.96, f32[1152,3456]{1,0:T(8,128)} %fusion.95), kind=kLoop, calls=%fused_computation | loop fusion | flops 23887872 | bytes 95551488 | tf_op jit(solution)/shard_map/concatenate | solution.py:184
  954.7 2.1 copy.90
  957.3 2.0 copy.93
  959.7 1.6 copy.91
  961.7 1.6 copy.92
  965.6 1.3 fusion.36
  966.9 73.4 %all-reduce.13 = (f32[1152]{0:T(1024)S(1)}, f32[256]{0:T(256)S(1)}, f32[256]{0:T(256)S(1)}, f32[1152]{0:T(1024)S(1)}, f32[1152]{0:T(1024)S(1)}, /*index=5*/f32[1152]{0:T(1024)S(1)}) all-reduce(f32[1152]{0:T(1024)S(1)} %get-tuple-element.25, f32[256]{0:T(256)S(1)} %copy-done.61, ...), channel_id=1, replica_groups=mesh['dp'=64,'tensor'=2] {'dp','tensor'}, use_global_device_ids=true, to_apply=%region_22.23 | all-reduce | flops 5120 | bytes 40960 | tf_op jit(solution)/shard_map/psum | solution.py:230
  1043.8 2.1 fusion.41
  1045.9 721.3 %all-reduce.20.cloned.1.call-done = (f32[589824]{0:T(1024)}, f32[294912]{0:T(1024)}, f32[294912]{0:T(1024)}, f32[589824]{0:T(1024)}, f32[1152,10368]{1,0:T(8,128)}) async-done(((f32[589824]{0:T(1024)}, f32[294912]{0:T(1024)}, f32[294912]{0:T(1024)}, f32[589824]{0:T(1024)}, f32[1152,10368]{1,0:T(8,128)}), (f32[589824]{0:T(1024)}, f32[294912]{0:T(1024)}, f32[294912]{0:T(1024)}, f32[589824]{0:T(1024)}, ...) | async-done | bytes 54853648
  1772.8 2.5 dynamic-slice_bitcast_fusion
  (251 shorter events, 33.9 us)
Async XLA Ops:
  20.6 12.6 copy-start.42
  20.6 12.6 copy-start.48
  20.6 12.6 copy-start.49
  20.6 13.4 copy-start.62
  20.6 15.2 copy-start.47
  20.6 15.5 copy-start.68
  20.6 15.7 copy-start.69
  20.6 15.9 copy-start.70
  20.6 16.2 copy-start.71
  20.6 579.2 %copy-start.6 = (bf16[128,1152]{1,0:T(8,128)(2,1)S(1)}, bf16[128,1152]{1,0:T(8,128)(2,1)}, u32[]{:S(2)}) copy-start(bf16[128,1152]{1,0:T(8,128)(2,1)} %param.16) | copy-start | bytes 884740
  20.7 680.5 %all-to-all-start = ((bf16[64,18,10370]{2,1,0:T(8,128)(2,1)}), bf16[64,18,10370]{2,1,0:T(8,128)(2,1)}, u32[]{:S(2)}, u32[]{:S(2)}) async-start(bf16[64,18,10370]{2,1,0:T(8,128)(2,1)} %stack.2), calls=%async_computation.1 | async-start | bytes 64487424 | tf_op jit(solution)/shard_map/all_to_all | solution.py:29
  32.4 585.9 %all-gather.7.cloned.1.call-start = ((), (), s32[]{:S(2)}) async-start(), calls=%async_computation.10 | async-start | bytes 1597440 | tf_op jit(solution)/shard_map/all_gather | solution.py:127
  33.1 588.2 %all-gather.5.cloned.1.call-start = ((), (), s32[]{:S(2)}) async-start(), calls=%async_computation.9 | async-start | bytes 3194880 | tf_op jit(solution)/shard_map/all_gather | solution.py:17
  33.9 664.6 %reduce-scatter.5.cloned.1.call-start = ((), (), s32[]{:S(2)}) async-start(), calls=%async_computation.5 | async-start | bytes 1769472 | tf_op jit(solution)/shard_map/reduce_scatter | solution.py:98
  36.0 585.3 %copy-start.44 = (f32[256]{0:T(256)}, f32[256]{0:T(256)S(1)}, u32[]{:S(2)}) copy-start(f32[256]{0:T(256)S(1)} %convert_element_type.128) | copy-start | bytes 3076
  598.5 37.9 %copy-start.50 = (f32[256]{0:T(256)}, f32[256]{0:T(256)S(1)}, u32[]{:S(2)}) copy-start(f32[256]{0:T(256)S(1)} %convert_element_type.130) | copy-start | bytes 3076
  598.5 31.9 %copy-start.51 = (f32[256]{0:T(256)}, f32[256]{0:T(256)S(1)}, u32[]{:S(2)}) copy-start(f32[256]{0:T(256)S(1)} %convert_element_type.127) | copy-start | bytes 3076
  599.8 21.5 %copy-start.54 = (f32[128]{0:T(128)}, f32[128]{0:T(128)S(1)}, u32[]{:S(2)}) copy-start(f32[128]{0:T(128)S(1)} %multiply_exponential_fusion) | copy-start | bytes 1540
  617.0 22.9 %copy-start.2 = (bf16[256,1152]{1,0:T(8,128)(2,1)}, bf16[256,1152]{1,0:T(8,128)(2,1)S(1)}, u32[]{:S(2)}) copy-start(bf16[256,1152]{1,0:T(8,128)(2,1)S(1)} %all_gather.31) | copy-start | bytes 1769476
  627.2 12.7 copy-start.4
  630.4 9.5 copy-start.43
  630.4 9.5 copy-start.35
  635.9 5.0 copy-start.22
  636.3 4.0 copy-start.17
  639.9 5.3 copy-start.37
  640.3 5.0 copy-start.59
  640.3 59.4 %copy-start.7 = (bf16[128,1152]{1,0:T(8,128)(2,1)S(1)}, bf16[128,1152]{1,0:T(8,128)(2,1)}, u32[]{:S(2)}) copy-start(bf16[128,1152]{1,0:T(8,128)(2,1)} %param.16) | copy-start | bytes 884740
  642.3 87.5 %copy-start.15 = (bf16[256,512]{1,0:T(8,128)(2,1)}, bf16[256,512]{1,0:T(8,128)(2,1)S(1)}, u32[]{:S(2)}) copy-start(bf16[256,512]{1,0:T(8,128)(2,1)S(1)} %reshape.368) | copy-start | bytes 786436
  645.2 144.9 %reduce-scatter.7.cloned.1.call-start = ((), (), s32[]{:S(2)}) async-start(), calls=%async_computation.6 | async-start | bytes 1769472 | tf_op jit(solution)/shard_map/reduce_scatter | solution.py:98
  645.3 55.8 %copy-start.33 = (f32[1152]{0:T(1024)}, f32[1152]{0:T(1024)S(1)}, u32[]{:S(2)}) copy-start(f32[1152]{0:T(1024)S(1)} %convert_element_type.135) | copy-start | bytes 13828
  699.7 30.1 %copy-start.52 = (f32[128]{0:T(128)}, f32[128]{0:T(128)S(1)}, u32[]{:S(2)}) copy-start(f32[128]{0:T(128)S(1)} %fusion.82) | copy-start | bytes 1540
  701.1 28.8 %copy-start.63 = (f32[128]{0:T(128)}, f32[128]{0:T(128)S(1)}, u32[]{:S(2)}) copy-start(f32[128]{0:T(128)S(1)} %get-tuple-element.47) | copy-start | bytes 1540
  701.1 30.8 %copy-start.55 = (f32[128]{0:T(128)}, f32[128]{0:T(128)S(1)}, u32[]{:S(2)}) copy-start(f32[128]{0:T(128)S(1)} %fusion.83) | copy-start | bytes 1540
  741.9 94.8 %copy-start.9 = (bf16[256,1152]{1,0:T(8,128)(2,1)}, bf16[256,1152]{1,0:T(8,128)(2,1)S(1)}, u32[]{:S(2)}) copy-start(bf16[256,1152]{1,0:T(8,128)(2,1)S(1)} %all_gather.37) | copy-start | bytes 1769476
  741.9 11.6 copy-start
  764.6 88.9 %reduce-scatter.9.cloned.1.call-start = ((), (), s32[]{:S(2)}) async-start(), calls=%async_computation.7 | async-start | bytes 1769472 | tf_op jit(solution)/shard_map/reduce_scatter | solution.py:98
  793.2 22.1 %slice-start = ((s8[24182784]{0:T(1024)(128)(4,1)}), s8[4194304]{0:T(1024)(128)(4,1)S(1)}, s32[]{:S(2)}) async-start(s8[24182784]{0:T(1024)(128)(4,1)} %bitcast.93), calls=%async_computation.13 | async-start | bytes 8388608
  804.9 10.4 copy-start.14
  804.9 10.4 slice-start.1
  804.9 10.4 slice-start.2
  804.9 10.4 slice-start.3
  804.9 11.7 slice-start.4
  804.9 12.6 slice-start.5
  826.7 86.4 %all-reduce.22.cloned.1.call-start = ((), (), s32[]{:S(2)}) async-start(), calls=%async_computation.12 | async-start | bytes 524288 | tf_op jit(solution)/shard_map/psum | solution.py:214
  826.9 9.8 copy-start.24
  836.7 7.9 copy-start.23
  844.6 11.6 copy-start.1
  853.6 4.8 copy-start.67
  853.6 4.8 copy-start.34
  853.6 4.8 copy-start.53
  853.6 14.9 copy-start.13
  858.3 10.8 copy-start.38
  869.0 8.3 copy-start.25
  869.1 9.1 copy-start.5
  869.1 9.1 copy-start.36
  877.3 36.8 %copy-start.45 = (f32[256]{0:T(256)S(1)}, f32[256]{0:T(256)}, u32[]{:S(2)}) copy-start(f32[256]{0:T(256)} %copy-done.44) | copy-start | bytes 3076
  881.9 83.7 %reduce-scatter.11.cloned.1.call-start = ((), (), s32[]{:S(2)}) async-start(), calls=%async_computation.8 | async-start | bytes 1769472 | tf_op jit(solution)/shard_map/reduce_scatter | solution.py:98
  913.1 6.7 copy-start.29
  921.2 33.0 %copy-start.3 = (bf16[256,1152]{1,0:T(8,128)(2,1)S(1)}, bf16[256,1152]{1,0:T(8,128)(2,1)}, u32[]{:S(2)}) copy-start(bf16[256,1152]{1,0:T(8,128)(2,1)} %copy-done.2) | copy-start | bytes 1769476
  921.2 33.0 %copy-start.18 = (bf16[256,2,256]{0,2,1:T(8,128)(2,1)S(1)}, bf16[256,2,256]{0,2,1:T(8,128)(2,1)}, u32[]{:S(2)}) copy-start(bf16[256,2,256]{0,2,1:T(8,128)(2,1)} %fusion.44) | copy-start | bytes 786436
  921.2 845.9 %all-reduce.20.cloned.1.call-start = ((), (), s32[]{:S(2)}) async-start(), calls=%async_computation.11 | async-start | bytes 109707264
  957.3 4.0 copy-start.30
  963.4 80.4 %copy-start.65 = (f32[128]{0:T(128)S(1)}, f32[128]{0:T(128)}, u32[]{:S(2)}) copy-start(f32[128]{0:T(128)} %copy-done.64) | copy-start | bytes 1540
  963.4 80.4 %copy-start.11 = (f32[128,1152]{1,0:T(8,128)S(1)}, f32[128,1152]{1,0:T(8,128)}, u32[]{:S(2)}) copy-start(f32[128,1152]{1,0:T(8,128)} %copy-done.10) | copy-start | bytes 1769476
  (23 other events, 39.8 us)
Sparse Core Ops, SparseCore 0:
  36.4 391.6 all-gather.6
  431.9 113.3 all-gather.4
  645.4 53.1 reduce-scatter.4
  764.8 25.2 reduce-scatter.6
  826.8 25.2 reduce-scatter.8
  882.0 31.0 all-reduce.21
  921.3 25.2 reduce-scatter.10
  963.6 803.5 all-reduce.19
